TPU v7x, 256 devices: a whole 4x4x8 slice. The times are simulated.
256 devices in a mesh: row: 16 (over z, y_hi), col: 16 (over y_lo, x, core).
Axes of the slice: x: 4, y: 4 (y_hi: 2, y_lo: 2; y = y_hi * 2 + y_lo), z: 8, core: 2. Of those that a mesh axis runs over, the one named last changes fastest.
Arguments:
- diag_block: float32 [2048, 2048], P('row'), as said below
- z_panel: float32 [2048, 2048], P('row', 'col'), may hold values from -0.046875 to 0.046875
- panel_below: float32 [32768, 2048], P('row', 'col'), may hold values from -6 to 6
- z_trail: float32 [32768, 2048], P('row', 'col'), may hold values from -6 to 6
- norm_sq: float32 [2048], P('col'), may hold values from 0.05 to 0.5
Outputs:
- norm_out: float32 [2048], P('col')
- trail_out: float32 [32768, 2048], P('row', 'col')
Inputs may be any that keep to these rules, and one draw needn't show every extreme that they name: diag_block is zero above its diagonal; its diagonal entries are at least 1.
All inputs are finite; a program needn't handle non-finite values.
Results may differ from a plain program's by a relative error of at most 0.00017.
Values sent between devices are 32-bit elements; how exact they have to be, the bound alone decides.
A program may use at most 64 MiB of HBM per device.

v0:
```python
import jax
import jax.numpy as jnp
from jax import lax
from jax.sharding import PartitionSpec as P


def copy_for_each(x, axis):
    copies = jnp.broadcast_to(x, (lax.axis_size(axis), *x.shape))
    return lax.all_to_all(copies, axis, split_axis=0, concat_axis=0, tiled=True)


def over_copies(x, axis):
    everything = copy_for_each(x, axis)
    return jnp.sum(everything, axis=0)


def shards(diag_block, z_panel, panel_below, z_trail, norm_sq):
    highest = lax.Precision.HIGHEST
    row_count = lax.axis_size("row")
    own_row = lax.axis_index("row")
    height = z_panel.shape[0]
    full_width = diag_block.shape[1]
    own_cols = z_panel.shape[1]
    identity = jnp.eye(height, dtype=jnp.float32)

    def advance(section, carry):
        solved, carried = carry
        diag_tile = lax.dynamic_slice_in_dim(diag_block, section * height, height, 1)
        is_owner = own_row == section
        pivot_tile = jnp.where(is_owner, diag_tile, identity)
        candidate = lax.linalg.triangular_solve(
            pivot_tile, z_panel - carried, left_side=True, lower=True
        )
        masked = jnp.where(is_owner, candidate, jnp.zeros_like(candidate))
        received = over_copies(masked, "row")
        carried = carried + jnp.dot(
            diag_tile, received, precision=highest, preferred_element_type=jnp.float32
        )
        solved = lax.dynamic_update_slice_in_dim(solved, received, section * height, 0)
        return (solved, carried)

    start_solved = jnp.zeros((full_width, own_cols), jnp.float32)
    start_carried = jnp.zeros((height, own_cols), jnp.float32)
    solved, unused_carry = lax.fori_loop(0, row_count, advance, (start_solved, start_carried))
    norm_out = norm_sq + jnp.sum(solved * solved, axis=0)
    update = jnp.dot(
        lax.all_gather(panel_below, "col", axis=1, tiled=True),
        solved,
        precision=highest,
        preferred_element_type=jnp.float32,
    )
    trail_out = z_trail - update
    return (norm_out, trail_out)


def solution(mesh):
    return jax.shard_map(
        shards,
        mesh=mesh,
        in_specs=(P("row", None), P("row", "col"), P("row", "col"), P("row", "col"), P("col")),
        out_specs=(P("col"), P("row", "col")),
        check_vma=False,
    )
```

profile of v0, /device:TPU:97, one launch (start us, length us, event | category | flops | bytes accessed | tf_op | source)
XLA Modules:
  0.0 800.5 jit_solution(2289007723152576863)
XLA Ops:
  9.6 760.9 %while.16 = (s32[]{:T(128)}, f32[2048,128]{1,0:T(8,128)S(1)}, f32[128,128]{1,0:T(8,128)S(1)}, s32[]{:T(128)}, f32[128,2048]{1,0:T(8,128)}, /*index=5*/f32[128,12...) while((s32[]{:T(128)}, f32[2048,128]{1,0:T(8,128)S(1)}, ...), condition=%wide.region_2.3_spmd.clone, body=%wide.region_0.2_spmd.clone.sunk | while | flops 50741256 | bytes 6160609 | solution.py:44
  10.5 9.8 %custom-call.10 = f32[1,128,128]{1,2,0:T(8,128)S(1)} custom-call(f32[1,128,128]{2,1,0:T(8,128)S(1)} %fusion.25), custom_call_target="InvertDiagBlocksLowerTriangular" | custom-call | tf_op jit(solution)/shard_map/while/body/eval_jaxpr/triangular_solve | solution.py:31
  32.2 28.6 %all-to-all-done = f32[16,128,128]{2,1,0:T(8,128)S(1)} async-done(((f32[16,128,128]{2,1,0:T(8,128)}), f32[16,128,128]{2,1,0:T(8,128)S(1)}, u32[]{:S(2)}, u32[]{:S(2)}) %all-to-all-start) | async-done | bytes 1048608 | tf_op jit(solution)/shard_map/while/body/eval_jaxpr/all_to_all | solution.py:9
  62.9 9.8 %custom-call.10 = f32[1,128,128]{1,2,0:T(8,128)S(1)} custom-call(f32[1,128,128]{2,1,0:T(8,128)S(1)} %fusion.25), custom_call_target="InvertDiagBlocksLowerTriangular" | custom-call | tf_op jit(solution)/shard_map/while/body/eval_jaxpr/triangular_solve | solution.py:31
  79.5 28.6 %all-to-all-done = f32[16,128,128]{2,1,0:T(8,128)S(1)} async-done(((f32[16,128,128]{2,1,0:T(8,128)}), f32[16,128,128]{2,1,0:T(8,128)S(1)}, u32[]{:S(2)}, u32[]{:S(2)}) %all-to-all-start) | async-done | bytes 1048608 | tf_op jit(solution)/shard_map/while/body/eval_jaxpr/all_to_all | solution.py:9
  110.1 9.8 %custom-call.10 = f32[1,128,128]{1,2,0:T(8,128)S(1)} custom-call(f32[1,128,128]{2,1,0:T(8,128)S(1)} %fusion.25), custom_call_target="InvertDiagBlocksLowerTriangular" | custom-call | tf_op jit(solution)/shard_map/while/body/eval_jaxpr/triangular_solve | solution.py:31
  126.7 28.6 %all-to-all-done = f32[16,128,128]{2,1,0:T(8,128)S(1)} async-done(((f32[16,128,128]{2,1,0:T(8,128)}), f32[16,128,128]{2,1,0:T(8,128)S(1)}, u32[]{:S(2)}, u32[]{:S(2)}) %all-to-all-start) | async-done | bytes 1048608 | tf_op jit(solution)/shard_map/while/body/eval_jaxpr/all_to_all | solution.py:9
  173.9 28.6 %all-to-all-done = f32[16,128,128]{2,1,0:T(8,128)S(1)} async-done(((f32[16,128,128]{2,1,0:T(8,128)}), f32[16,128,128]{2,1,0:T(8,128)S(1)}, u32[]{:S(2)}, u32[]{:S(2)}) %all-to-all-start) | async-done | bytes 1048608 | tf_op jit(solution)/shard_map/while/body/eval_jaxpr/all_to_all | solution.py:9
  221.2 28.6 %all-to-all-done = f32[16,128,128]{2,1,0:T(8,128)S(1)} async-done(((f32[16,128,128]{2,1,0:T(8,128)}), f32[16,128,128]{2,1,0:T(8,128)S(1)}, u32[]{:S(2)}, u32[]{:S(2)}) %all-to-all-start) | async-done | bytes 1048608 | tf_op jit(solution)/shard_map/while/body/eval_jaxpr/all_to_all | solution.py:9
  251.8 9.8 %custom-call.10 = f32[1,128,128]{1,2,0:T(8,128)S(1)} custom-call(f32[1,128,128]{2,1,0:T(8,128)S(1)} %fusion.25), custom_call_target="InvertDiagBlocksLowerTriangular" | custom-call | tf_op jit(solution)/shard_map/while/body/eval_jaxpr/triangular_solve | solution.py:31
  268.4 28.6 %all-to-all-done = f32[16,128,128]{2,1,0:T(8,128)S(1)} async-done(((f32[16,128,128]{2,1,0:T(8,128)}), f32[16,128,128]{2,1,0:T(8,128)S(1)}, u32[]{:S(2)}, u32[]{:S(2)}) %all-to-all-start) | async-done | bytes 1048608 | tf_op jit(solution)/shard_map/while/body/eval_jaxpr/all_to_all | solution.py:9
  315.6 28.6 %all-to-all-done = f32[16,128,128]{2,1,0:T(8,128)S(1)} async-done(((f32[16,128,128]{2,1,0:T(8,128)}), f32[16,128,128]{2,1,0:T(8,128)S(1)}, u32[]{:S(2)}, u32[]{:S(2)}) %all-to-all-start) | async-done | bytes 1048608 | tf_op jit(solution)/shard_map/while/body/eval_jaxpr/all_to_all | solution.py:9
  362.9 28.6 %all-to-all-done = f32[16,128,128]{2,1,0:T(8,128)S(1)} async-done(((f32[16,128,128]{2,1,0:T(8,128)}), f32[16,128,128]{2,1,0:T(8,128)S(1)}, u32[]{:S(2)}, u32[]{:S(2)}) %all-to-all-start) | async-done | bytes 1048608 | tf_op jit(solution)/shard_map/while/body/eval_jaxpr/all_to_all | solution.py:9
  410.1 28.6 %all-to-all-done = f32[16,128,128]{2,1,0:T(8,128)S(1)} async-done(((f32[16,128,128]{2,1,0:T(8,128)}), f32[16,128,128]{2,1,0:T(8,128)S(1)}, u32[]{:S(2)}, u32[]{:S(2)}) %all-to-all-start) | async-done | bytes 1048608 | tf_op jit(solution)/shard_map/while/body/eval_jaxpr/all_to_all | solution.py:9
  457.3 28.6 %all-to-all-done = f32[16,128,128]{2,1,0:T(8,128)S(1)} async-done(((f32[16,128,128]{2,1,0:T(8,128)}), f32[16,128,128]{2,1,0:T(8,128)S(1)}, u32[]{:S(2)}, u32[]{:S(2)}) %all-to-all-start) | async-done | bytes 1048608 | tf_op jit(solution)/shard_map/while/body/eval_jaxpr/all_to_all | solution.py:9
  504.5 28.6 %all-to-all-done = f32[16,128,128]{2,1,0:T(8,128)S(1)} async-done(((f32[16,128,128]{2,1,0:T(8,128)}), f32[16,128,128]{2,1,0:T(8,128)S(1)}, u32[]{:S(2)}, u32[]{:S(2)}) %all-to-all-start) | async-done | bytes 1048608 | tf_op jit(solution)/shard_map/while/body/eval_jaxpr/all_to_all | solution.py:9
  535.2 9.8 %custom-call.10 = f32[1,128,128]{1,2,0:T(8,128)S(1)} custom-call(f32[1,128,128]{2,1,0:T(8,128)S(1)} %fusion.25), custom_call_target="InvertDiagBlocksLowerTriangular" | custom-call | tf_op jit(solution)/shard_map/while/body/eval_jaxpr/triangular_solve | solution.py:31
  551.8 28.6 %all-to-all-done = f32[16,128,128]{2,1,0:T(8,128)S(1)} async-done(((f32[16,128,128]{2,1,0:T(8,128)}), f32[16,128,128]{2,1,0:T(8,128)S(1)}, u32[]{:S(2)}, u32[]{:S(2)}) %all-to-all-start) | async-done | bytes 1048608 | tf_op jit(solution)/shard_map/while/body/eval_jaxpr/all_to_all | solution.py:9
  582.4 9.8 %custom-call.10 = f32[1,128,128]{1,2,0:T(8,128)S(1)} custom-call(f32[1,128,128]{2,1,0:T(8,128)S(1)} %fusion.25), custom_call_target="InvertDiagBlocksLowerTriangular" | custom-call | tf_op jit(solution)/shard_map/while/body/eval_jaxpr/triangular_solve | solution.py:31
  599.0 28.6 %all-to-all-done = f32[16,128,128]{2,1,0:T(8,128)S(1)} async-done(((f32[16,128,128]{2,1,0:T(8,128)}), f32[16,128,128]{2,1,0:T(8,128)S(1)}, u32[]{:S(2)}, u32[]{:S(2)}) %all-to-all-start) | async-done | bytes 1048608 | tf_op jit(solution)/shard_map/while/body/eval_jaxpr/all_to_all | solution.py:9
  646.2 28.6 %all-to-all-done = f32[16,128,128]{2,1,0:T(8,128)S(1)} async-done(((f32[16,128,128]{2,1,0:T(8,128)}), f32[16,128,128]{2,1,0:T(8,128)S(1)}, u32[]{:S(2)}, u32[]{:S(2)}) %all-to-all-start) | async-done | bytes 1048608 | tf_op jit(solution)/shard_map/while/body/eval_jaxpr/all_to_all | solution.py:9
  693.5 28.6 %all-to-all-done = f32[16,128,128]{2,1,0:T(8,128)S(1)} async-done(((f32[16,128,128]{2,1,0:T(8,128)}), f32[16,128,128]{2,1,0:T(8,128)S(1)}, u32[]{:S(2)}, u32[]{:S(2)}) %all-to-all-start) | async-done | bytes 1048608 | tf_op jit(solution)/shard_map/while/body/eval_jaxpr/all_to_all | solution.py:9
  740.7 28.6 %all-to-all-done = f32[16,128,128]{2,1,0:T(8,128)S(1)} async-done(((f32[16,128,128]{2,1,0:T(8,128)}), f32[16,128,128]{2,1,0:T(8,128)S(1)}, u32[]{:S(2)}, u32[]{:S(2)}) %all-to-all-start) | async-done | bytes 1048608 | tf_op jit(solution)/shard_map/while/body/eval_jaxpr/all_to_all | solution.py:9
  771.3 21.0 %fusion.12 = f32[2048,128]{0,1:T(8,128)S(1)} fusion(f32[2048,128]{0,1:T(8,128)S(1)} %copy.9, f32[2048,128]{1,0:T(8,128)S(1)} %get-tuple-element.126, f32[2048,2048]{1,0:T(8,128)} %all-gather.2.cloned.1.call-done), kind=kOutput, calls=%fused_computation.18 | convolution fusion | flops 6442713088 | bytes 19922944 | tf_op jit(solution)/shard_map/dot_general | solution.py:46
  (133 shorter events, 247.7 us)
Async XLA Ops:
  7.2 763.6 %copy-start = (f32[128]{0:T(128)S(1)}, f32[128]{0:T(128)}, u32[]{:S(2)}) copy-start(f32[128]{0:T(128)} %param.11) | copy-start | bytes 1540
  7.2 764.1 %all-gather.2.cloned.1.call-start = ((), (), s32[]{:S(2)}) async-start(), calls=%async_computation.1 | async-start | bytes 17825792 | tf_op jit(solution)/shard_map/all_gather | solution.py:47
  22.5 38.4 %all-to-all-start = ((f32[16,128,128]{2,1,0:T(8,128)}), f32[16,128,128]{2,1,0:T(8,128)S(1)}, u32[]{:S(2)}, u32[]{:S(2)}) async-start(f32[16,128,128]{2,1,0:T(8,128)} %broadcast_in_dim.13), calls=%async_computation | async-start | bytes 2097152 | tf_op jit(solution)/shard_map/while/body/eval_jaxpr/all_to_all | solution.py:9
  74.9 33.2 %all-to-all-start = ((f32[16,128,128]{2,1,0:T(8,128)}), f32[16,128,128]{2,1,0:T(8,128)S(1)}, u32[]{:S(2)}, u32[]{:S(2)}) async-start(f32[16,128,128]{2,1,0:T(8,128)} %broadcast_in_dim.13), calls=%async_computation | async-start | bytes 2097152 | tf_op jit(solution)/shard_map/while/body/eval_jaxpr/all_to_all | solution.py:9
  122.2 33.2 %all-to-all-start = ((f32[16,128,128]{2,1,0:T(8,128)}), f32[16,128,128]{2,1,0:T(8,128)S(1)}, u32[]{:S(2)}, u32[]{:S(2)}) async-start(f32[16,128,128]{2,1,0:T(8,128)} %broadcast_in_dim.13), calls=%async_computation | async-start | bytes 2097152 | tf_op jit(solution)/shard_map/while/body/eval_jaxpr/all_to_all | solution.py:9
  169.4 33.2 %all-to-all-start = ((f32[16,128,128]{2,1,0:T(8,128)}), f32[16,128,128]{2,1,0:T(8,128)S(1)}, u32[]{:S(2)}, u32[]{:S(2)}) async-start(f32[16,128,128]{2,1,0:T(8,128)} %broadcast_in_dim.13), calls=%async_computation | async-start | bytes 2097152 | tf_op jit(solution)/shard_map/while/body/eval_jaxpr/all_to_all | solution.py:9
  216.6 33.2 %all-to-all-start = ((f32[16,128,128]{2,1,0:T(8,128)}), f32[16,128,128]{2,1,0:T(8,128)S(1)}, u32[]{:S(2)}, u32[]{:S(2)}) async-start(f32[16,128,128]{2,1,0:T(8,128)} %broadcast_in_dim.13), calls=%async_computation | async-start | bytes 2097152 | tf_op jit(solution)/shard_map/while/body/eval_jaxpr/all_to_all | solution.py:9
  263.8 33.2 %all-to-all-start = ((f32[16,128,128]{2,1,0:T(8,128)}), f32[16,128,128]{2,1,0:T(8,128)S(1)}, u32[]{:S(2)}, u32[]{:S(2)}) async-start(f32[16,128,128]{2,1,0:T(8,128)} %broadcast_in_dim.13), calls=%async_computation | async-start | bytes 2097152 | tf_op jit(solution)/shard_map/while/body/eval_jaxpr/all_to_all | solution.py:9
  311.1 33.2 %all-to-all-start = ((f32[16,128,128]{2,1,0:T(8,128)}), f32[16,128,128]{2,1,0:T(8,128)S(1)}, u32[]{:S(2)}, u32[]{:S(2)}) async-start(f32[16,128,128]{2,1,0:T(8,128)} %broadcast_in_dim.13), calls=%async_computation | async-start | bytes 2097152 | tf_op jit(solution)/shard_map/while/body/eval_jaxpr/all_to_all | solution.py:9
  358.3 33.2 %all-to-all-start = ((f32[16,128,128]{2,1,0:T(8,128)}), f32[16,128,128]{2,1,0:T(8,128)S(1)}, u32[]{:S(2)}, u32[]{:S(2)}) async-start(f32[16,128,128]{2,1,0:T(8,128)} %broadcast_in_dim.13), calls=%async_computation | async-start | bytes 2097152 | tf_op jit(solution)/shard_map/while/body/eval_jaxpr/all_to_all | solution.py:9
  405.5 33.2 %all-to-all-start = ((f32[16,128,128]{2,1,0:T(8,128)}), f32[16,128,128]{2,1,0:T(8,128)S(1)}, u32[]{:S(2)}, u32[]{:S(2)}) async-start(f32[16,128,128]{2,1,0:T(8,128)} %broadcast_in_dim.13), calls=%async_computation | async-start | bytes 2097152 | tf_op jit(solution)/shard_map/while/body/eval_jaxpr/all_to_all | solution.py:9
  452.8 33.2 %all-to-all-start = ((f32[16,128,128]{2,1,0:T(8,128)}), f32[16,128,128]{2,1,0:T(8,128)S(1)}, u32[]{:S(2)}, u32[]{:S(2)}) async-start(f32[16,128,128]{2,1,0:T(8,128)} %broadcast_in_dim.13), calls=%async_computation | async-start | bytes 2097152 | tf_op jit(solution)/shard_map/while/body/eval_jaxpr/all_to_all | solution.py:9
  500.0 33.2 %all-to-all-start = ((f32[16,128,128]{2,1,0:T(8,128)}), f32[16,128,128]{2,1,0:T(8,128)S(1)}, u32[]{:S(2)}, u32[]{:S(2)}) async-start(f32[16,128,128]{2,1,0:T(8,128)} %broadcast_in_dim.13), calls=%async_computation | async-start | bytes 2097152 | tf_op jit(solution)/shard_map/while/body/eval_jaxpr/all_to_all | solution.py:9
  547.2 33.2 %all-to-all-start = ((f32[16,128,128]{2,1,0:T(8,128)}), f32[16,128,128]{2,1,0:T(8,128)S(1)}, u32[]{:S(2)}, u32[]{:S(2)}) async-start(f32[16,128,128]{2,1,0:T(8,128)} %broadcast_in_dim.13), calls=%async_computation | async-start | bytes 2097152 | tf_op jit(solution)/shard_map/while/body/eval_jaxpr/all_to_all | solution.py:9
  594.4 33.2 %all-to-all-start = ((f32[16,128,128]{2,1,0:T(8,128)}), f32[16,128,128]{2,1,0:T(8,128)S(1)}, u32[]{:S(2)}, u32[]{:S(2)}) async-start(f32[16,128,128]{2,1,0:T(8,128)} %broadcast_in_dim.13), calls=%async_computation | async-start | bytes 2097152 | tf_op jit(solution)/shard_map/while/body/eval_jaxpr/all_to_all | solution.py:9
  641.7 33.2 %all-to-all-start = ((f32[16,128,128]{2,1,0:T(8,128)}), f32[16,128,128]{2,1,0:T(8,128)S(1)}, u32[]{:S(2)}, u32[]{:S(2)}) async-start(f32[16,128,128]{2,1,0:T(8,128)} %broadcast_in_dim.13), calls=%async_computation | async-start | bytes 2097152 | tf_op jit(solution)/shard_map/while/body/eval_jaxpr/all_to_all | solution.py:9
  688.9 33.2 %all-to-all-start = ((f32[16,128,128]{2,1,0:T(8,128)}), f32[16,128,128]{2,1,0:T(8,128)S(1)}, u32[]{:S(2)}, u32[]{:S(2)}) async-start(f32[16,128,128]{2,1,0:T(8,128)} %broadcast_in_dim.13), calls=%async_computation | async-start | bytes 2097152 | tf_op jit(solution)/shard_map/while/body/eval_jaxpr/all_to_all | solution.py:9
  736.1 33.2 %all-to-all-start = ((f32[16,128,128]{2,1,0:T(8,128)}), f32[16,128,128]{2,1,0:T(8,128)S(1)}, u32[]{:S(2)}, u32[]{:S(2)}) async-start(f32[16,128,128]{2,1,0:T(8,128)} %broadcast_in_dim.13), calls=%async_computation | async-start | bytes 2097152 | tf_op jit(solution)/shard_map/while/body/eval_jaxpr/all_to_all | solution.py:9
Sparse Core Ops, SparseCore 0:
  9.8 121.2 all-gather.1
where the time goes:
time: 807 us; the launch traced here: 800 us
  waiting for transfers between devices  458 us (57%)
  other arithmetic  172 us (21%)
  starting transfers between devices  78.1 us (10%)
  matrix products  56.1 us (7%)
  local copies, waits for them, and re-layouts  20.3 us (3%)
  between operations  14.1 us (2%)
    all_to_all x16, waiting for transfers between devices, copy_for_each(): return lax.all_to_all(copies, axis, split_axis=0, concat_axis=0, tiled=True)  458 us
    another operation x32, other arithmetic, advance(): lax.linalg.triangular_solve(pivot_tile, z_panel - carried, left_side=True...  171 us
    all_to_all x16, starting transfers between devices, copy_for_each(): return lax.all_to_all(copies, axis, split_axis=0, concat_axis=0, tiled=True)  78.1 us
    dot_general x1, matrix products, shards(): jnp.dot(lax.all_gather(panel_below, 'col', axis=1, tiled=True), solved, p...  21 us
    another operation x16, matrix products, advance(): lax.linalg.triangular_solve(pivot_tile, z_panel - carried, left_side=True...  18 us
    broadcast_in_dim x16, local copies, waits for them, and re-layouts, copy_for_each(): copies = jnp.broadcast_to(x, (lax.axis_size(axis), *x.shape))  17.2 us
    dot_general x16, matrix products, advance(): jnp.dot(diag_tile, received, precision=highest, preferred_element_type=jn...  17.1 us
  transfers between devices with their start and end apart: 17, of which 16 were waited for; matrix products, arithmetic and copies ran while one was open for 28% of the time, Pallas kernels for 0%

commit v1 on v0

v1 whole, which is shorter than its diff:
```python
import jax
import jax.numpy as jnp
from jax import lax
from jax.experimental import pallas as pl
from jax.experimental.pallas import tpu as pltpu
from jax.sharding import PartitionSpec as P

F32 = jnp.float32
BF16 = jnp.bfloat16
T = 128
PIECES = 4


def halves(v):
    high = v.astype(BF16)
    low = (v - high.astype(F32)).astype(BF16)
    return high, low


def left_form(v):
    high, low = halves(v)
    return jnp.concatenate([high, low], axis=1)


def right_form(v):
    high, low = halves(v)
    both = jnp.concatenate([high, low], axis=1)
    return jnp.concatenate([both, both], axis=0)


def product(left, right):
    wide = jnp.dot(left, right, preferred_element_type=F32)
    return wide[:, :T] + wide[:, T:]


def invert_lower(blocks):
    rows = lax.broadcasted_iota(jnp.int32, (T, T), 0)
    cols = lax.broadcasted_iota(jnp.int32, (T, T), 1)
    on_diag = rows == cols
    found = [jnp.where(on_diag, 1.0 / jnp.where(on_diag, b, 1.0), 0.0) for b in blocks]
    size = 1
    while size < T:
        below = (
            (rows // (2 * size) == cols // (2 * size))
            & ((rows // size) % 2 == 1)
            & ((cols // size) % 2 == 0)
        )
        offs = [jnp.where(below, b, 0.0) for b in blocks]
        mids = [product(left_form(o), right_form(x)) for o, x in zip(offs, found)]
        found = [x - product(left_form(x), right_form(m)) for x, m in zip(found, mids)]
        size *= 2
    return found


def kernel(
    d_hbm, z_hbm, a_hbm, norm_ref,
    norm_out, update_ref,
    panel, lower, zbuf, acc, solved, solved_right, inverse,
    own_sem, send_a, recv_a, send_l, recv_l, send_z, recv_z, send_s, recv_s,
):
    row = lax.axis_index("row")
    col = lax.axis_index("col")
    z, hi = row // 2, row % 2
    lo, x, core = col // 8, (col // 2) % 4, col % 2
    height = a_hbm.shape[0]
    piece_rows = height // PIECES
    planes = 8

    def place(lo_, x_, core_):
        return lo_ * 8 + x_ * 2 + core_

    x_next, x_prev, x_far = (x + 1) % 4, (x + 3) % 4, (x + 2) % 4
    to_x_next = {"row": row, "col": place(lo, x_next, core)}
    to_x_prev = {"row": row, "col": place(lo, x_prev, core)}
    to_y = {"row": row, "col": place(1 - lo, x, core)}
    to_sibling = {"row": row, "col": place(lo, x, 1 - core)}
    to_pair_l = {"row": z * 2 + 1 - hi, "col": place(1 - lo, x, core)}
    to_pair_z = {"row": z * 2 + 1 - hi, "col": col}
    to_z_next = {"row": ((z + 1) % planes) * 2 + hi, "col": col}
    to_z_prev = {"row": ((z + planes - 1) % planes) * 2 + hi, "col": col}
    partners = [to_x_next, to_x_prev, to_y, to_sibling, to_pair_l, to_pair_z, to_z_next, to_z_prev]

    own_copies = [pltpu.make_async_copy(a_hbm, panel.at[col], own_sem.at[0])]
    own_copies.append(pltpu.make_async_copy(z_hbm, zbuf.at[hi], own_sem.at[1]))
    for j in range(planes):
        own_copies.append(
            pltpu.make_async_copy(d_hbm.at[:, pl.ds(2 * T * j, 2 * T)], lower.at[hi, j], own_sem.at[2 + j])
        )
    for c in own_copies:
        c.start()

    barrier = pltpu.get_barrier_semaphore()
    for d in partners:
        pl.semaphore_signal(barrier, inc=1, device_id=d, device_id_type=pl.DeviceIdType.MESH)
    pl.semaphore_wait(barrier, len(partners))

    def remote(src, dst, s, r, target):
        return pltpu.make_async_remote_copy(
            src_ref=src, dst_ref=dst, send_sem=s, recv_sem=r,
            device_id=target, device_id_type=pl.DeviceIdType.MESH,
        )

    def lower_copy(j):
        return remote(
            d_hbm.at[:, pl.ds(2 * T * j, 2 * T)], lower.at[hi, j], send_l.at[j], recv_l.at[j], to_pair_l
        )

    def lower_arrived(j):
        remote(lower.at[1 - hi, j], lower.at[1 - hi, j], send_l.at[j], recv_l.at[j], to_pair_l).wait_recv()

    for j in range(planes):
        @pl.when(z == j)
        def _():
            lower_copy(j).start()
    z_copy = remote(z_hbm, zbuf.at[hi], send_z.at[0], recv_z.at[0], to_pair_z)
    z_copy.start()
    for j in range(planes):
        @pl.when(z > j)
        def _():
            lower_copy(j).start()

    pending = []
    arrived = set()

    def span(p):
        return pl.ds(p * piece_rows, piece_rows)

    def send_panel(src, slot, p, target):
        c = remote(src, panel.at[slot, span(p)], send_a.at[len(pending)], recv_a.at[slot, p], target)
        c.start()
        pending.append(c)

    slots = {
        (side, where): place(side_lo, where_x, core)
        for side, side_lo in (("own", lo), ("other", 1 - lo))
        for where, where_x in (("here", x), ("prev", x_prev), ("next", x_next), ("far", x_far))
    }

    def wait_panel(slot, p):
        view = panel.at[slot, span(p)]
        remote(view, view, send_a.at[0], recv_a.at[slot, p], to_sibling).wait_recv()

    def receive(key, p):
        if (key, p) in arrived:
            return
        arrived.add((key, p))
        slot = slots[key]
        wait_panel(slot, p)
        send_panel(panel.at[slot, span(p)], slot, p, to_sibling)

    def forward(key, p, target):
        receive(key, p)
        slot = slots[key]
        send_panel(panel.at[slot, span(p)], slot, p, target)

    for p, q in zip((0, 2, 1, 3), (2, 3, 0, 1)):
        send_panel(a_hbm.at[span(p)], col, p, to_x_next)
        send_panel(a_hbm.at[span(p)], col, p, to_x_prev)
        send_panel(a_hbm.at[span(q)], col, q, to_y)
        send_panel(a_hbm.at[span(p)], col, p, to_sibling)

    def relay_1():
        forward(("own", "prev"), 0, to_x_next)
        forward(("own", "prev"), 0, to_y)
        forward(("own", "next"), 0, to_y)
        forward(("other", "here"), 2, to_x_next)
        forward(("other", "here"), 2, to_x_prev)

    def relay_2():
        forward(("own", "next"), 1, to_x_prev)
        forward(("other", "here"), 3, to_x_next)
        forward(("other", "here"), 3, to_x_prev)
        forward(("own", "prev"), 1, to_y)
        forward(("own", "next"), 1, to_y)

    def relay_3():
        forward(("own", "prev"), 2, to_x_next)
        forward(("own", "next"), 3, to_x_prev)

    def relay_4():
        forward(("own", "far"), 0, to_y)
        forward(("own", "far"), 1, to_y)

    def relay_5():
        forward(("other", "prev"), 2, to_x_next)
        forward(("other", "next"), 3, to_x_prev)

    relays = {1: relay_1, 3: relay_2, 4: relay_3, 5: relay_4, 6: relay_5}

    for c in own_copies:
        c.wait()
    z_copy.wait_send()
    remote(zbuf.at[1 - hi], zbuf.at[1 - hi], send_z.at[0], recv_z.at[0], to_pair_z).wait_recv()
    for j in range(planes):
        @pl.when(z == j)
        def _():
            lower_arrived(j)
    acc[...] = zbuf[...].reshape(2 * T, T)
    first_rows = lower[0, z]
    second_rows = lower[1, z]
    inv_a, inv_b = invert_lower([first_rows[:, :T], second_rows[:, T:]])
    inverse[0] = left_form(inv_a)
    inverse[1] = left_form(inv_b)
    inverse[2] = left_form(second_rows[:, :T])

    def solved_copy(k, half, target, way):
        view = solved.at[2 * k + half]
        return remote(view, view, send_s.at[way, 2 * k + half], recv_s.at[2 * k + half], target)

    for k in range(planes):
        dist = (z - k + planes) % planes
        goes_next = dist <= 3
        goes_prev = (dist == 0) | (dist >= 6)

        def spread(half):
            @pl.when(goes_next)
            def _():
                solved_copy(k, half, to_z_next, 0).start()

            @pl.when(goes_prev)
            def _():
                solved_copy(k, half, to_z_prev, 1).start()

        @pl.when(dist == 0)
        def _():
            s_a = product(inverse[0], right_form(acc[:T]))
            solved[2 * k] = s_a
            spread(0)
            rest = acc[T:] - product(inverse[2], right_form(s_a))
            solved[2 * k + 1] = product(inverse[1], right_form(rest))
            spread(1)

        @pl.when(dist != 0)
        def _():
            @pl.when(z > k)
            def _():
                lower_arrived(k)

            tile = lower[:, k].reshape(2 * T, 2 * T)
            for half in range(2):
                solved_copy(k, half, to_z_next, 0).wait_recv()
                spread(half)

                @pl.when(z > k)
                def _():
                    acc[...] -= product(
                        left_form(tile[:, half * T:(half + 1) * T]), right_form(solved[2 * k + half])
                    )

        if k in relays:
            relays[k]()

    for p in range(PIECES):
        for key in slots:
            if key != ("own", "here"):
                receive(key, p)
    for p in range(PIECES):
        for lo_ in range(2):
            for x_ in range(4):
                wait_panel(place(lo_, x_, 1 - core), p)

    total = norm_ref[...]
    for k in range(2 * planes):
        block = solved[k]
        total = total + jnp.sum(block * block, axis=0, keepdims=True)
        solved_right[k] = right_form(block)
    norm_out[...] = total

    tile_rows = 512

    def multiply(i, carry):
        pair, t = i // (height // tile_rows), i % (height // tile_rows)
        part = pl.ds(pl.multiple_of(t * tile_rows, tile_rows), tile_rows)
        left = jnp.concatenate([left_form(panel[2 * pair, part]), left_form(panel[2 * pair + 1, part])], axis=1)
        right = solved_right[pl.ds(2 * pair, 2)].reshape(4 * T, 2 * T)
        value = product(left, right)

        @pl.when(pair == 0)
        def _():
            update_ref[part] = value

        @pl.when(pair > 0)
        def _():
            update_ref[part] += value

        return carry

    lax.fori_loop(0, planes * (height // tile_rows), multiply, 0)

    for c in pending:
        c.wait_send()
    for j in range(planes):
        @pl.when(z >= j)
        def _():
            lower_copy(j).wait_send()
    for k in range(planes):
        dist = (z - k + planes) % planes
        for half in range(2):
            @pl.when(dist <= 3)
            def _():
                solved_copy(k, half, to_z_next, 0).wait_send()

            @pl.when((dist == 0) | (dist >= 6))
            def _():
                solved_copy(k, half, to_z_prev, 1).wait_send()


def shards(diag_block, z_panel, panel_below, z_trail, norm_sq):
    height = panel_below.shape[0]
    dma = pltpu.SemaphoreType.DMA
    norm_out, update = pl.pallas_call(
        kernel,
        out_shape=(
            jax.ShapeDtypeStruct((1, T), F32),
            jax.ShapeDtypeStruct((height, T), F32),
        ),
        in_specs=[pl.BlockSpec(memory_space=pl.ANY)] * 3 + [pl.BlockSpec(memory_space=pltpu.VMEM)],
        out_specs=(pl.BlockSpec(memory_space=pltpu.VMEM),) * 2,
        scratch_shapes=[
            pltpu.VMEM((16, height, T), F32),
            pltpu.VMEM((2, 8, T, 2 * T), F32),
            pltpu.VMEM((2, T, T), F32),
            pltpu.VMEM((2 * T, T), F32),
            pltpu.VMEM((16, T, T), F32),
            pltpu.VMEM((16, 2 * T, 2 * T), BF16),
            pltpu.VMEM((3, T, 2 * T), BF16),
            dma((10,)), dma((64,)), dma((16, PIECES)), dma((8,)), dma((8,)),
            dma((1,)), dma((1,)), dma((2, 16)), dma((16,)),
        ],
        compiler_params=pltpu.CompilerParams(
            collective_id=0, has_side_effects=True, vmem_limit_bytes=48 * 1024 * 1024
        ),
        name="panel_update",
    )(diag_block, z_panel, panel_below, norm_sq.reshape(1, T))
    return norm_out.reshape(T), z_trail - update


def solution(mesh):
    return jax.shard_map(
        shards,
        mesh=mesh,
        in_specs=(P("row", None), P("row", "col"), P("row", "col"), P("row", "col"), P("col")),
        out_specs=(P("col"), P("row", "col")),
        check_vma=False,
    )
```

time: 807 us -> 104 us (0.13)
  waiting for transfers between devices: 458 us -> 0 us
  other arithmetic: 172 us -> 1.08 us
  Pallas kernels: 0 us -> 97.5 us
  starting transfers between devices: 78.1 us -> 0 us
  matrix products: 56.1 us -> 0 us
  local copies, waits for them, and re-layouts: 20.3 us -> 4.45 us
  between operations: 14.1 us -> 0.66 us
    all_to_all x16 -> x0, waiting for transfers between devices: 458 us -> none  [copy_for_each(): return lax.all_to_all(copies, axis, split_axis=0, concat_axis=0, tiled=True)]
    another operation x32 -> x0, other arithmetic: 171 us -> none  [advance(): lax.linalg.triangular_solve(pivot_tile, z_panel - carried, left_side=True...]
    pallas_call x0 -> x1, Pallas kernels: none -> 97.5 us  [shards(): pl.pallas_call(kernel, out_shape=(jax.ShapeDtypeStruct((1, T), F32), jax....]
    all_to_all x16 -> x0, starting transfers between devices: 78.1 us -> none  [copy_for_each(): return lax.all_to_all(copies, axis, split_axis=0, concat_axis=0, tiled=True)]
    dot_general x17 -> x0, matrix products: 38.1 us -> none  [the longest x1 21 us: shards(): jnp.dot(lax.all_gather(panel_below, 'col', axis=1, tiled=True), solved, p...]
    another operation x16 -> x0, matrix products: 18 us -> none  [advance(): lax.linalg.triangular_solve(pivot_tile, z_panel - carried, left_side=True...]
    broadcast_in_dim x17 -> x0, local copies, waits for them, and re-layouts: 17.2 us -> none  [the longest x16 17.2 us: copy_for_each(): copies = jnp.broadcast_to(x, (lax.axis_size(axis), *x.shape))]
  transfers between devices with their start and end apart: 17 -> 0, of which waited for: 16 -> 0; matrix products, arithmetic and copies ran while one was open for 28% -> 0% of each run, Pallas kernels for 0% -> 0%
where the time goes in v1:
time: 104 us
  Pallas kernels  97.5 us (94%)
  local copies, waits for them, and re-layouts  4.45 us (4%)
  other arithmetic  1.08 us (1%)
    pallas_call x1, Pallas kernels, shards(): pl.pallas_call(kernel, out_shape=(jax.ShapeDtypeStruct((1, T), F32), jax....  97.5 us
    unnamed x11, local copies, waits for them, and re-layouts  4.45 us

profile of v1, /device:TPU:97, one launch (start us, length us, event | category | flops | bytes accessed | tf_op | source)
XLA Modules:
  0.0 103.7 jit_solution(15041281561427417622)
XLA Ops:
  0.6 0.0 copy-start.3
  0.6 0.6 copy-done.3
  1.3 0.0 copy-start
  1.3 1.2 %copy-done = f32[128,2048]{1,0:T(8,128)S(1)} copy-done((f32[128,2048]{1,0:T(8,128)S(1)}, f32[128,2048]{1,0:T(8,128)}, u32[]{:S(2)}) %copy-start) | copy-done | bytes 1048600
  2.5 0.0 copy-start.1
  2.5 1.2 %copy-done.1 = f32[2048,128]{1,0:T(8,128)S(1)} copy-done((f32[2048,128]{1,0:T(8,128)S(1)}, f32[2048,128]{1,0:T(8,128)}, u32[]{:S(2)}) %copy-start.1) | copy-done | bytes 1048600
  3.7 0.0 copy-start.2
  3.7 0.8 copy-done.2
  4.6 0.0 copy-start.4
  4.6 97.5 %panel_update.1 = (f32[1,128]{1,0:T(1,128)S(1)}, f32[2048,128]{1,0:T(8,128)S(1)}) custom-call(f32[128,2048]{1,0:T(8,128)S(1)} %copy-done, f32[128,128]{1,0:T(8,128)S(1)} %copy-done.2, f32[2048,128]{1,0:T(8,128)S(1)} %copy-done.1, f32[1,128]{1,0:T(1,128)S(1)} %bitcast.2), custom_call_target="tpu_custom_call" | custom-call | tf_op jit(solution)/shard_map/panel_update/pallas_call | solution.py:311
  102.1 0.0 copy-done.4
  102.1 1.1 %sub.3 = f32[2048,128]{1,0:T(8,128)} subtract(f32[2048,128]{1,0:T(8,128)S(1)} %copy-done.4, f32[2048,128]{1,0:T(8,128)S(1)} %get-tuple-element.5) | non-fusion elementwise | flops 262144 | bytes 3145728 | tf_op jit(solution)/shard_map/sub | solution.py:335
  103.2 0.5 copy.8
Async XLA Ops:
  0.6 0.7 copy-start.3
  1.3 1.2 %copy-start = (f32[128,2048]{1,0:T(8,128)S(1)}, f32[128,2048]{1,0:T(8,128)}, u32[]{:S(2)}) copy-start(f32[128,2048]{1,0:T(8,128)} %d_hbm.1) | copy-start | bytes 3145732
  2.5 1.2 %copy-start.1 = (f32[2048,128]{1,0:T(8,128)S(1)}, f32[2048,128]{1,0:T(8,128)}, u32[]{:S(2)}) copy-start(f32[2048,128]{1,0:T(8,128)} %a_hbm.1) | copy-start | bytes 3145732
  3.7 0.8 copy-start.2
  4.6 97.5 %copy-start.4 = (f32[2048,128]{1,0:T(8,128)S(1)}, f32[2048,128]{1,0:T(8,128)}, u32[]{:S(2)}) copy-start(f32[2048,128]{1,0:T(8,128)} %param.8) | copy-start | bytes 3145732

commit v2 on v1

--- a/solution.py
+++ b/solution.py
@@ -153,39 +153,81 @@
         slot = slots[key]
         send_panel(panel.at[slot, span(p)], slot, p, target)
 
-    for p, q in zip((0, 2, 1, 3), (2, 3, 0, 1)):
+    for p, q, y in zip((0, 2, 1, 3), (1, 3, 0, 2), (2, 3, 0, 1)):
         send_panel(a_hbm.at[span(p)], col, p, to_x_next)
-        send_panel(a_hbm.at[span(p)], col, p, to_x_prev)
-        send_panel(a_hbm.at[span(q)], col, q, to_y)
+        send_panel(a_hbm.at[span(q)], col, q, to_x_prev)
+        send_panel(a_hbm.at[span(y)], col, y, to_y)
         send_panel(a_hbm.at[span(p)], col, p, to_sibling)
 
-    def relay_1():
-        forward(("own", "prev"), 0, to_x_next)
-        forward(("own", "prev"), 0, to_y)
-        forward(("own", "next"), 0, to_y)
-        forward(("other", "here"), 2, to_x_next)
-        forward(("other", "here"), 2, to_x_prev)
-
-    def relay_2():
-        forward(("own", "next"), 1, to_x_prev)
-        forward(("other", "here"), 3, to_x_next)
-        forward(("other", "here"), 3, to_x_prev)
-        forward(("own", "prev"), 1, to_y)
-        forward(("own", "next"), 1, to_y)
-
-    def relay_3():
-        forward(("own", "prev"), 2, to_x_next)
-        forward(("own", "next"), 3, to_x_prev)
-
-    def relay_4():
-        forward(("own", "far"), 0, to_y)
-        forward(("own", "far"), 1, to_y)
-
-    def relay_5():
-        forward(("other", "prev"), 2, to_x_next)
-        forward(("other", "next"), 3, to_x_prev)
-
-    relays = {1: relay_1, 3: relay_2, 4: relay_3, 5: relay_4, 6: relay_5}
+    prev, following, far = ("own", "prev"), ("own", "next"), ("own", "far")
+    across, across_prev, across_next = ("other", "here"), ("other", "prev"), ("other", "next")
+    relays = {
+        1: (
+            [(prev, 0, to_x_next), (following, 1, to_x_prev), (across, 2, to_x_next),
+             (prev, 0, to_y), (following, 1, to_y)],
+            [],
+        ),
+        2: (
+            [(across, 3, to_x_prev), (across, 2, to_x_prev), (across, 3, to_x_next),
+             (prev, 2, to_x_next), (following, 3, to_x_prev)],
+            [],
+        ),
+        3: ([(prev, 1, to_y), (following, 0, to_y)], [(across, 0)]),
+        4: ([(far, 0, to_y), (far, 1, to_y)], [(prev, 3), (following, 2), (across, 1)]),
+        5: ([(across_prev, 2, to_x_next), (across_next, 3, to_x_prev)], [(across_prev, 0)]),
+        6: ([], [(across_prev, 3), (across_next, 2), (across_next, 1), (across_prev, 1)]),
+    }
+
+    def relay(k):
+        onward, taken = relays.get(k, ([], []))
+        for key, p, target in onward:
+            forward(key, p, target)
+        for key, p in taken:
+            receive(key, p)
+
+    sibling_taken = set()
+
+    def wait_sibling(key):
+        if key in sibling_taken:
+            return
+        sibling_taken.add(key)
+        for p in range(PIECES):
+            wait_panel(slots[key] + 1 - 2 * core, p)
+
+    tile_rows = 512
+    chip = lo * 4 + x
+
+    def multiply(pair):
+        right = solved_right[pl.ds(2 * pair, 2)].reshape(4 * T, 2 * T)
+
+        def tile(t, carry):
+            part = pl.ds(pl.multiple_of(t * tile_rows, tile_rows), tile_rows)
+            left = jnp.concatenate(
+                [left_form(panel[2 * pair, part]), left_form(panel[2 * pair + 1, part])], axis=1
+            )
+            update_ref[part] += product(left, right)
+            return carry
+
+        lax.fori_loop(0, height // tile_rows, tile, 0)
+
+    def step_of(pair):
+        same_plane = pair // 4 == lo
+        apart = (pair % 4 - x + 4) % 4
+        near = jnp.where(same_plane, apart != 2, apart == 0)
+        here = same_plane & (apart == 0)
+        phase = jnp.where(here, 1, jnp.where(near, 5, planes))
+        due = jnp.maximum(pair, phase)
+        return due + jnp.where(z == due + 1, 1, 0)
+
+    def multiply_due(k):
+        def one(pair, carry):
+            @pl.when(step_of(pair) == k)
+            def _():
+                multiply(pair)
+
+            return carry
+
+        lax.fori_loop(0, planes, one, 0)
 
     for c in own_copies:
         c.wait()
@@ -196,6 +238,7 @@
         def _():
             lower_arrived(j)
     acc[...] = zbuf[...].reshape(2 * T, T)
+    update_ref[...] = jnp.zeros_like(update_ref)
     first_rows = lower[0, z]
     second_rows = lower[1, z]
     inv_a, inv_b = invert_lower([first_rows[:, :T], second_rows[:, T:]])
@@ -247,45 +290,29 @@
                         left_form(tile[:, half * T:(half + 1) * T]), right_form(solved[2 * k + half])
                     )
 
-        if k in relays:
-            relays[k]()
+        for half in range(2):
+            solved_right[2 * k + half] = right_form(solved[2 * k + half])
+        relay(k)
+        if k == 1:
+            wait_sibling(("own", "here"))
+        if k == 5:
+            for key in (prev, following, across):
+                wait_sibling(key)
+        if k >= 1:
+            multiply_due(k)
 
     for p in range(PIECES):
         for key in slots:
             if key != ("own", "here"):
                 receive(key, p)
-    for p in range(PIECES):
-        for lo_ in range(2):
-            for x_ in range(4):
-                wait_panel(place(lo_, x_, 1 - core), p)
-
+    for key in slots:
+        wait_sibling(key)
+    multiply_due(planes)
     total = norm_ref[...]
     for k in range(2 * planes):
         block = solved[k]
         total = total + jnp.sum(block * block, axis=0, keepdims=True)
-        solved_right[k] = right_form(block)
     norm_out[...] = total
-
-    tile_rows = 512
-
-    def multiply(i, carry):
-        pair, t = i // (height // tile_rows), i % (height // tile_rows)
-        part = pl.ds(pl.multiple_of(t * tile_rows, tile_rows), tile_rows)
-        left = jnp.concatenate([left_form(panel[2 * pair, part]), left_form(panel[2 * pair + 1, part])], axis=1)
-        right = solved_right[pl.ds(2 * pair, 2)].reshape(4 * T, 2 * T)
-        value = product(left, right)
-
-        @pl.when(pair == 0)
-        def _():
-            update_ref[part] = value
-
-        @pl.when(pair > 0)
-        def _():
-            update_ref[part] += value
-
-        return carry
-
-    lax.fori_loop(0, planes * (height // tile_rows), multiply, 0)
 
     for c in pending:
         c.wait_send()
@@ -328,7 +355,7 @@
             dma((1,)), dma((1,)), dma((2, 16)), dma((16,)),
         ],
         compiler_params=pltpu.CompilerParams(
-            collective_id=0, has_side_effects=True, vmem_limit_bytes=48 * 1024 * 1024
+            collective_id=0, has_side_effects=True, vmem_limit_bytes=67_043_328
         ),
         name="panel_update",
     )(diag_block, z_panel, panel_below, norm_sq.reshape(1, T))

time: 104 us -> 94.8 us (0.912)
  Pallas kernels: 97.5 us -> 90.8 us
  local copies, waits for them, and re-layouts: 4.45 us -> 0.52 us
  other arithmetic: 1.08 us -> 2.62 us
    pallas_call x1, Pallas kernels: 97.5 us -> 90.8 us  [shards(): pl.pallas_call(kernel, out_shape=(jax.ShapeDtypeStruct((1, T), F32), jax....]
    unnamed x11 -> x3, local copies, waits for them, and re-layouts: 4.45 us -> 0.52 us
    sub x1, other arithmetic: 1.08 us -> 2.62 us  [shards(): return (norm_out.reshape(T), z_trail - update)]
where the time goes in v2:
time: 94.8 us; the launch traced here: 94.6 us
  Pallas kernels  90.8 us (96%)
  other arithmetic  2.62 us (3%)
    pallas_call x1, Pallas kernels, shards(): pl.pallas_call(kernel, out_shape=(jax.ShapeDtypeStruct((1, T), F32), jax....  90.8 us
    sub x1, other arithmetic, shards(): return (norm_out.reshape(T), z_trail - update)  2.62 us

profile of v2, /device:TPU:97, one launch (start us, length us, event | category | flops | bytes accessed | tf_op | source)
XLA Modules:
  0.0 94.6 jit_solution(8564207646675338683)
XLA Ops:
  0.6 90.8 %panel_update.1 = (f32[1,128]{1,0:T(1,128)}, f32[2048,128]{1,0:T(8,128)}) custom-call(f32[128,2048]{1,0:T(8,128)} %d_hbm.1, f32[128,128]{1,0:T(8,128)} %z_hbm.1, f32[2048,128]{1,0:T(8,128)} %a_hbm.1, f32[1,128]{1,0:T(1,128)} %bitcast.2), custom_call_target="tpu_custom_call" | custom-call | tf_op jit(solution)/shard_map/panel_update/pallas_call | solution.py:338
  91.4 0.0 copy-start
  91.4 2.6 %sub.3 = f32[2048,128]{1,0:T(8,128)} subtract(f32[2048,128]{1,0:T(8,128)} %param.8, f32[2048,128]{1,0:T(8,128)} %get-tuple-element.5) | non-fusion elementwise | flops 262144 | bytes 3145728 | tf_op jit(solution)/shard_map/sub | solution.py:362
  94.0 0.0 copy-done
  94.0 0.5 copy.8
Async XLA Ops:
  91.4 2.6 %copy-start = (f32[1,128]{1,0:T(1,128)S(1)}, f32[1,128]{1,0:T(1,128)}, u32[]{:S(2)}) copy-start(f32[1,128]{1,0:T(1,128)} %get-tuple-element.4) | copy-start | bytes 1540

commit v3 on v2

--- a/solution.py
+++ b/solution.py
@@ -52,6 +52,34 @@
     return found
 
 
+def relay_table(planes):
+    windows = ((9.5, 21.0), (15.0, 21.0), (21.0, 33.0), (31.0, 43.0), (36.5, 43.0), (48.0, 55.0))
+    starts = (6.4, 4.7, 2.2, 0.0, 7.4, 10.5, 14.1, 12.3)
+
+    def reached(k, z):
+        apart = (z - k) % planes
+        return 14.4 + 5.4 * k + 3.1 * min(apart, planes - apart)
+
+    table, first = [], [0] * planes
+    for ready, limit in windows:
+        steps = []
+        for z in range(planes):
+            there = ready + starts[z] + 3.0
+            slack = 0.8 * (max(starts) - starts[z])
+
+            def cost(k):
+                when = reached(k, z)
+                late = 0.3 * max(when - there, 0.0) + max(when - limit - starts[z] - slack, 0.0)
+                if k < z - 1:
+                    late += 6.0 * max(there + 1.0 - reached(z - 1, z), 0.0)
+                return late + 0.3 * max(there - when, 0.0)
+
+            steps.append(min(range(first[z], planes), key=cost))
+        first = steps
+        table.append(steps)
+    return table
+
+
 def kernel(
     d_hbm, z_hbm, a_hbm, norm_ref,
     norm_out, update_ref,
@@ -120,15 +148,16 @@
             lower_copy(j).start()
 
     pending = []
-    arrived = set()
 
     def span(p):
         return pl.ds(p * piece_rows, piece_rows)
 
-    def send_panel(src, slot, p, target):
-        c = remote(src, panel.at[slot, span(p)], send_a.at[len(pending)], recv_a.at[slot, p], target)
-        c.start()
-        pending.append(c)
+    def panel_copy(src, slot, p, index, target):
+        return remote(src, panel.at[slot, span(p)], send_a.at[index], recv_a.at[slot, p], target)
+
+    def send_own(p, target):
+        panel_copy(a_hbm.at[span(p)], col, p, len(pending), target).start()
+        pending.append((col, p, target))
 
     slots = {
         (side, where): place(side_lo, where_x, core)
@@ -140,59 +169,85 @@
         view = panel.at[slot, span(p)]
         remote(view, view, send_a.at[0], recv_a.at[slot, p], to_sibling).wait_recv()
 
-    def receive(key, p):
-        if (key, p) in arrived:
-            return
-        arrived.add((key, p))
-        slot = slots[key]
-        wait_panel(slot, p)
-        send_panel(panel.at[slot, span(p)], slot, p, to_sibling)
-
-    def forward(key, p, target):
-        receive(key, p)
-        slot = slots[key]
-        send_panel(panel.at[slot, span(p)], slot, p, target)
-
     for p, q, y in zip((0, 2, 1, 3), (1, 3, 0, 2), (2, 3, 0, 1)):
-        send_panel(a_hbm.at[span(p)], col, p, to_x_next)
-        send_panel(a_hbm.at[span(q)], col, q, to_x_prev)
-        send_panel(a_hbm.at[span(y)], col, y, to_y)
-        send_panel(a_hbm.at[span(p)], col, p, to_sibling)
+        send_own(p, to_x_next)
+        send_own(q, to_x_prev)
+        send_own(y, to_y)
+        send_own(p, to_sibling)
 
     prev, following, far = ("own", "prev"), ("own", "next"), ("own", "far")
     across, across_prev, across_next = ("other", "here"), ("other", "prev"), ("other", "next")
-    relays = {
-        1: (
+    every = range(PIECES)
+    groups = [
+        (
             [(prev, 0, to_x_next), (following, 1, to_x_prev), (across, 2, to_x_next),
              (prev, 0, to_y), (following, 1, to_y)],
-            [],
-        ),
-        2: (
+            [], [("own", "here")],
+        ),
+        (
             [(across, 3, to_x_prev), (across, 2, to_x_prev), (across, 3, to_x_next),
              (prev, 2, to_x_next), (following, 3, to_x_prev)],
-            [],
-        ),
-        3: ([(prev, 1, to_y), (following, 0, to_y)], [(across, 0)]),
-        4: ([(far, 0, to_y), (far, 1, to_y)], [(prev, 3), (following, 2), (across, 1)]),
-        5: ([(across_prev, 2, to_x_next), (across_next, 3, to_x_prev)], [(across_prev, 0)]),
-        6: ([], [(across_prev, 3), (across_next, 2), (across_next, 1), (across_prev, 1)]),
-    }
-
-    def relay(k):
-        onward, taken = relays.get(k, ([], []))
-        for key, p, target in onward:
-            forward(key, p, target)
-        for key, p in taken:
-            receive(key, p)
-
-    sibling_taken = set()
-
-    def wait_sibling(key):
-        if key in sibling_taken:
-            return
-        sibling_taken.add(key)
-        for p in range(PIECES):
-            wait_panel(slots[key] + 1 - 2 * core, p)
+            [], [],
+        ),
+        ([(prev, 1, to_y), (following, 0, to_y)], [(across, 0)], []),
+        ([(far, 0, to_y), (far, 1, to_y)], [(prev, 3), (following, 2), (across, 1)], []),
+        (
+            [(across_prev, 2, to_x_next), (across_next, 3, to_x_prev)],
+            [(across_prev, 0), (across_next, 1)], [prev, following, across],
+        ),
+        (
+            [], [(across_prev, 3), (across_next, 2), (across_prev, 1), (far, 2), (far, 3)],
+            [far, across_prev],
+        ),
+        ([], [(("other", "far"), p) for p in (0, 2, 3, 1)] + [(across_next, 0)], [across_next, ("other", "far")]),
+    ]
+    plans = []
+    arrived = set()
+    for onward, taken, beside in groups:
+        plan = []
+        for key, p, target in onward + [(key, p, None) for key, p in taken]:
+            if (key, p) not in arrived:
+                arrived.add((key, p))
+                plan.append((slots[key], p, None, None))
+                plan.append((slots[key], p, len(pending), to_sibling))
+                pending.append((slots[key], p, to_sibling))
+            if target is not None:
+                plan.append((slots[key], p, len(pending), target))
+                pending.append((slots[key], p, target))
+        plans.append((plan, beside))
+
+    def relay(group):
+        plan, beside = plans[group]
+        for slot, p, index, target in plan:
+            if target is None:
+                wait_panel(slot, p)
+            else:
+                panel_copy(panel.at[slot, span(p)], slot, p, index, target).start()
+        for key in beside:
+            for p in every:
+                wait_panel(slots[key] + 1 - 2 * core, p)
+
+    relay_steps = relay_table(planes)
+
+    def by_plane(values):
+        picked = jnp.int32(values[0])
+        for v in range(1, planes):
+            picked = jnp.where(z == v, values[v], picked)
+        return picked
+
+    def relay_due(k):
+        for group, steps in enumerate(relay_steps):
+            here = [v for v in range(planes) if steps[v] == k]
+            if len(here) == planes:
+                relay(group)
+            elif here:
+                chosen = z == here[0]
+                for v in here[1:]:
+                    chosen = chosen | (z == v)
+
+                @pl.when(chosen)
+                def _():
+                    relay(group)
 
     tile_rows = 512
     chip = lo * 4 + x
@@ -200,24 +255,24 @@
     def multiply(pair):
         right = solved_right[pl.ds(2 * pair, 2)].reshape(4 * T, 2 * T)
 
-        def tile(t, carry):
-            part = pl.ds(pl.multiple_of(t * tile_rows, tile_rows), tile_rows)
+        for t in range(height // tile_rows):
+            part = pl.ds(t * tile_rows, tile_rows)
             left = jnp.concatenate(
                 [left_form(panel[2 * pair, part]), left_form(panel[2 * pair + 1, part])], axis=1
             )
             update_ref[part] += product(left, right)
-            return carry
-
-        lax.fori_loop(0, height // tile_rows, tile, 0)
 
     def step_of(pair):
         same_plane = pair // 4 == lo
         apart = (pair % 4 - x + 4) % 4
         near = jnp.where(same_plane, apart != 2, apart == 0)
+        middle = jnp.where(same_plane, apart == 2, apart == 3)
         here = same_plane & (apart == 0)
-        phase = jnp.where(here, 1, jnp.where(near, 5, planes))
+        phase = jnp.where(middle, by_plane(relay_steps[5]), planes)
+        phase = jnp.where(near, by_plane(relay_steps[4]), phase)
+        phase = jnp.where(here, by_plane(relay_steps[0]), phase)
         due = jnp.maximum(pair, phase)
-        return due + jnp.where(z == due + 1, 1, 0)
+        return due
 
     def multiply_due(k):
         def one(pair, carry):
@@ -250,63 +305,65 @@
         view = solved.at[2 * k + half]
         return remote(view, view, send_s.at[way, 2 * k + half], recv_s.at[2 * k + half], target)
 
+    def spread(k, half):
+        dist = (z - k + planes) % planes
+
+        @pl.when(dist <= 3)
+        def _():
+            solved_copy(k, half, to_z_next, 0).start()
+
+        @pl.when((dist == 0) | (dist >= 6))
+        def _():
+            solved_copy(k, half, to_z_prev, 1).start()
+
+    def solve_own(k, rest_a, rest_b):
+        s_a = product(inverse[0], right_form(rest_a))
+        solved[2 * k] = s_a
+        spread(k, 0)
+        solved[2 * k + 1] = product(inverse[1], right_form(rest_b() - product(inverse[2], right_form(s_a))))
+        spread(k, 1)
+
+    @pl.when(z == 0)
+    def _():
+        solve_own(0, acc[:T], lambda: acc[T:])
+
     for k in range(planes):
-        dist = (z - k + planes) % planes
-        goes_next = dist <= 3
-        goes_prev = (dist == 0) | (dist >= 6)
-
-        def spread(half):
-            @pl.when(goes_next)
+        @pl.when(z > k)
+        def _():
+            lower_arrived(k)
+            tile = lower[:, k].reshape(2 * T, 2 * T)
+            solved_copy(k, 0, to_z_next, 0).wait_recv()
+            spread(k, 0)
+            acc[...] -= product(left_form(tile[:, :T]), right_form(solved[2 * k]))
+            solved_copy(k, 1, to_z_next, 0).wait_recv()
+            spread(k, 1)
+            right = right_form(solved[2 * k + 1])
+
+            @pl.when(z == k + 1)
             def _():
-                solved_copy(k, half, to_z_next, 0).start()
-
-            @pl.when(goes_prev)
+                if k + 1 < planes:
+                    solve_own(
+                        k + 1,
+                        acc[:T] - product(left_form(tile[:T, T:]), right),
+                        lambda: acc[T:] - product(left_form(tile[T:, T:]), right),
+                    )
+
+            @pl.when(z > k + 1)
             def _():
-                solved_copy(k, half, to_z_prev, 1).start()
-
-        @pl.when(dist == 0)
-        def _():
-            s_a = product(inverse[0], right_form(acc[:T]))
-            solved[2 * k] = s_a
-            spread(0)
-            rest = acc[T:] - product(inverse[2], right_form(s_a))
-            solved[2 * k + 1] = product(inverse[1], right_form(rest))
-            spread(1)
-
-        @pl.when(dist != 0)
-        def _():
-            @pl.when(z > k)
-            def _():
-                lower_arrived(k)
-
-            tile = lower[:, k].reshape(2 * T, 2 * T)
+                acc[...] -= product(left_form(tile[:, T:]), right)
+
+        @pl.when(z < k)
+        def _():
             for half in range(2):
                 solved_copy(k, half, to_z_next, 0).wait_recv()
-                spread(half)
-
-                @pl.when(z > k)
-                def _():
-                    acc[...] -= product(
-                        left_form(tile[:, half * T:(half + 1) * T]), right_form(solved[2 * k + half])
-                    )
+                spread(k, half)
 
         for half in range(2):
             solved_right[2 * k + half] = right_form(solved[2 * k + half])
-        relay(k)
-        if k == 1:
-            wait_sibling(("own", "here"))
-        if k == 5:
-            for key in (prev, following, across):
-                wait_sibling(key)
-        if k >= 1:
-            multiply_due(k)
-
-    for p in range(PIECES):
-        for key in slots:
-            if key != ("own", "here"):
-                receive(key, p)
-    for key in slots:
-        wait_sibling(key)
+        relay_due(k)
+        multiply_due(k)
+
+    relay(len(groups) - 1)
     multiply_due(planes)
     total = norm_ref[...]
     for k in range(2 * planes):
@@ -314,8 +371,8 @@
         total = total + jnp.sum(block * block, axis=0, keepdims=True)
     norm_out[...] = total
 
-    for c in pending:
-        c.wait_send()
+    for index, (slot, p, target) in enumerate(pending):
+        panel_copy(panel.at[slot, span(p)], slot, p, index, target).wait_send()
     for j in range(planes):
         @pl.when(z >= j)
         def _():

time: 94.8 us -> 88.4 us (0.932)
  Pallas kernels: 90.8 us -> 83.9 us
    pallas_call x1, Pallas kernels: 90.8 us -> 83.9 us  [shards(): pl.pallas_call(kernel, out_shape=(jax.ShapeDtypeStruct((1, T), F32), jax....]
where the time goes in v3:
time: 88.4 us; the launch traced here: 87.7 us
  Pallas kernels  83.9 us (95%)
  other arithmetic  2.62 us (3%)
    pallas_call x1, Pallas kernels, shards(): pl.pallas_call(kernel, out_shape=(jax.ShapeDtypeStruct((1, T), F32), jax....  83.9 us
    sub x1, other arithmetic, shards(): return (norm_out.reshape(T), z_trail - update)  2.62 us

profile of v3, /device:TPU:97, one launch (start us, length us, event | category | flops | bytes accessed | tf_op | source)
XLA Modules:
  0.0 87.7 jit_solution(5663148160510509771)
XLA Ops:
  0.6 83.9 %panel_update.1 = (f32[1,128]{1,0:T(1,128)}, f32[2048,128]{1,0:T(8,128)}) custom-call(f32[128,2048]{1,0:T(8,128)} %d_hbm.1, f32[128,128]{1,0:T(8,128)} %z_hbm.1, f32[2048,128]{1,0:T(8,128)} %a_hbm.1, f32[1,128]{1,0:T(1,128)} %bitcast.2), custom_call_target="tpu_custom_call" | custom-call | tf_op jit(solution)/shard_map/panel_update/pallas_call | solution.py:395
  84.5 0.0 copy-start
  84.5 2.6 %sub.3 = f32[2048,128]{1,0:T(8,128)} subtract(f32[2048,128]{1,0:T(8,128)} %param.8, f32[2048,128]{1,0:T(8,128)} %get-tuple-element.5) | non-fusion elementwise | flops 262144 | bytes 3145728 | tf_op jit(solution)/shard_map/sub | solution.py:419
  87.2 0.0 copy-done
  87.2 0.5 copy.8
Async XLA Ops:
  84.5 2.6 %copy-start = (f32[1,128]{1,0:T(1,128)S(1)}, f32[1,128]{1,0:T(1,128)}, u32[]{:S(2)}) copy-start(f32[1,128]{1,0:T(1,128)} %get-tuple-element.4) | copy-start | bytes 1540

commit v4 on v3

--- a/solution.py
+++ b/solution.py
@@ -84,7 +84,7 @@
     d_hbm, z_hbm, a_hbm, norm_ref,
     norm_out, update_ref,
     panel, lower, zbuf, acc, solved, solved_right, inverse,
-    own_sem, send_a, recv_a, send_l, recv_l, send_z, recv_z, send_s, recv_s,
+    own_sem, send_a, recv_a, send_l, recv_l, send_z, recv_z, send_s, recv_s, send_d,
 ):
     row = lax.axis_index("row")
     col = lax.axis_index("col")
@@ -120,7 +120,16 @@
     barrier = pltpu.get_barrier_semaphore()
     for d in partners:
         pl.semaphore_signal(barrier, inc=1, device_id=d, device_id_type=pl.DeviceIdType.MESH)
-    pl.semaphore_wait(barrier, len(partners))
+    last = planes - 1
+    opposite = 3
+
+    @pl.when(z == opposite)
+    def _():
+        pl.semaphore_signal(
+            barrier, inc=1, device_id={"row": 2 * last + hi, "col": col}, device_id_type=pl.DeviceIdType.MESH
+        )
+
+    pl.semaphore_wait(barrier, len(partners) + jnp.where(z == last, 1, 0))
 
     def remote(src, dst, s, r, target):
         return pltpu.make_async_remote_copy(
@@ -305,16 +314,27 @@
         view = solved.at[2 * k + half]
         return remote(view, view, send_s.at[way, 2 * k + half], recv_s.at[2 * k + half], target)
 
+    def direct_copy(half):
+        view = solved.at[2 * last + half]
+        target = {"row": 2 * opposite + hi, "col": col}
+        return remote(view, view, send_d.at[half], recv_s.at[2 * last + half], target)
+
     def spread(k, half):
         dist = (z - k + planes) % planes
 
-        @pl.when(dist <= 3)
+        @pl.when(dist <= (3 if k < last else 2))
         def _():
             solved_copy(k, half, to_z_next, 0).start()
 
         @pl.when((dist == 0) | (dist >= 6))
         def _():
             solved_copy(k, half, to_z_prev, 1).start()
+
+        if k == last and half == 1:
+            @pl.when(dist == 0)
+            def _():
+                direct_copy(0).start()
+                direct_copy(1).start()
 
     def solve_own(k, rest_a, rest_b):
         s_a = product(inverse[0], right_form(rest_a))
@@ -380,9 +400,14 @@
     for k in range(planes):
         dist = (z - k + planes) % planes
         for half in range(2):
-            @pl.when(dist <= 3)
+            @pl.when(dist <= (3 if k < last else 2))
             def _():
                 solved_copy(k, half, to_z_next, 0).wait_send()
+
+            if k == last:
+                @pl.when(dist == 0)
+                def _():
+                    direct_copy(half).wait_send()
 
             @pl.when((dist == 0) | (dist >= 6))
             def _():
@@ -409,7 +434,7 @@
             pltpu.VMEM((16, 2 * T, 2 * T), BF16),
             pltpu.VMEM((3, T, 2 * T), BF16),
             dma((10,)), dma((64,)), dma((16, PIECES)), dma((8,)), dma((8,)),
-            dma((1,)), dma((1,)), dma((2, 16)), dma((16,)),
+            dma((1,)), dma((1,)), dma((2, 16)), dma((16,)), dma((2,)),
         ],
         compiler_params=pltpu.CompilerParams(
             collective_id=0, has_side_effects=True, vmem_limit_bytes=67_043_328

time: 88.4 us -> 87 us (0.984)
  the two profiles are of different devices: /device:TPU:97 before, /device:TPU:68 now
where the time goes in v4:
time: 87 us; the launch traced here: 86.8 us
  Pallas kernels  83 us (95%)
  other arithmetic  2.62 us (3%)
    pallas_call x1, Pallas kernels, shards(): pl.pallas_call(kernel, out_shape=(jax.ShapeDtypeStruct((1, T), F32), jax....  83 us
    sub x1, other arithmetic, shards(): return (norm_out.reshape(T), z_trail - update)  2.62 us

profile of v4, /device:TPU:68, one launch (start us, length us, event | category | flops | bytes accessed | tf_op | source)
XLA Modules:
  0.0 86.8 jit_solution(15048360417723592337)
XLA Ops:
  0.6 83.0 %panel_update.1 = (f32[1,128]{1,0:T(1,128)}, f32[2048,128]{1,0:T(8,128)}) custom-call(f32[128,2048]{1,0:T(8,128)} %d_hbm.1, f32[128,128]{1,0:T(8,128)} %z_hbm.1, f32[2048,128]{1,0:T(8,128)} %a_hbm.1, f32[1,128]{1,0:T(1,128)} %bitcast.2), custom_call_target="tpu_custom_call" | custom-call | tf_op jit(solution)/shard_map/panel_update/pallas_call | solution.py:420
  83.7 0.0 copy-start
  83.7 2.6 %sub.3 = f32[2048,128]{1,0:T(8,128)} subtract(f32[2048,128]{1,0:T(8,128)} %param.8, f32[2048,128]{1,0:T(8,128)} %get-tuple-element.5) | non-fusion elementwise | flops 262144 | bytes 3145728 | tf_op jit(solution)/shard_map/sub | solution.py:444
  86.3 0.0 copy-done
  86.3 0.5 copy.8
Async XLA Ops:
  83.7 2.6 %copy-start = (f32[1,128]{1,0:T(1,128)S(1)}, f32[1,128]{1,0:T(1,128)}, u32[]{:S(2)}) copy-start(f32[1,128]{1,0:T(1,128)} %get-tuple-element.4) | copy-start | bytes 1540

commit v5 on v4

--- a/solution.py
+++ b/solution.py
@@ -322,11 +322,11 @@
     def spread(k, half):
         dist = (z - k + planes) % planes
 
-        @pl.when(dist <= (3 if k < last else 2))
+        @pl.when(dist <= (3 if k < last else 1))
         def _():
             solved_copy(k, half, to_z_next, 0).start()
 
-        @pl.when((dist == 0) | (dist >= 6))
+        @pl.when((dist == 0) | (dist >= 6) | (dist == (4 if k == last else 0)))
         def _():
             solved_copy(k, half, to_z_prev, 1).start()
 
@@ -400,7 +400,7 @@
     for k in range(planes):
         dist = (z - k + planes) % planes
         for half in range(2):
-            @pl.when(dist <= (3 if k < last else 2))
+            @pl.when(dist <= (3 if k < last else 1))
             def _():
                 solved_copy(k, half, to_z_next, 0).wait_send()
 
@@ -409,7 +409,7 @@
                 def _():
                     direct_copy(half).wait_send()
 
-            @pl.when((dist == 0) | (dist >= 6))
+            @pl.when((dist == 0) | (dist >= 6) | (dist == (4 if k == last else 0)))
             def _():
                 solved_copy(k, half, to_z_prev, 1).wait_send()
 

time: 87 us -> 84.8 us (0.975)
  the two profiles are of different devices: /device:TPU:68 before, /device:TPU:36 now
where the time goes in v5:
time: 84.8 us; the launch traced here: 84.6 us
  Pallas kernels  80.9 us (95%)
  other arithmetic  2.62 us (3%)
    pallas_call x1, Pallas kernels, shards(): pl.pallas_call(kernel, out_shape=(jax.ShapeDtypeStruct((1, T), F32), jax....  80.9 us
    sub x1, other arithmetic, shards(): return (norm_out.reshape(T), z_trail - update)  2.62 us

profile of v5, /device:TPU:36, one launch (start us, length us, event | category | flops | bytes accessed | tf_op | source)
XLA Modules:
  0.0 84.6 jit_solution(10522398322324873480)
XLA Ops:
  0.6 80.9 %panel_update.1 = (f32[1,128]{1,0:T(1,128)}, f32[2048,128]{1,0:T(8,128)}) custom-call(f32[128,2048]{1,0:T(8,128)} %d_hbm.1, f32[128,128]{1,0:T(8,128)} %z_hbm.1, f32[2048,128]{1,0:T(8,128)} %a_hbm.1, f32[1,128]{1,0:T(1,128)} %bitcast.2), custom_call_target="tpu_custom_call" | custom-call | tf_op jit(solution)/shard_map/panel_update/pallas_call | solution.py:420
  81.5 0.0 copy-start
  81.5 2.6 %sub.3 = f32[2048,128]{1,0:T(8,128)} subtract(f32[2048,128]{1,0:T(8,128)} %param.8, f32[2048,128]{1,0:T(8,128)} %get-tuple-element.5) | non-fusion elementwise | flops 262144 | bytes 3145728 | tf_op jit(solution)/shard_map/sub | solution.py:444
  84.1 0.0 copy-done
  84.1 0.5 copy.8
Async XLA Ops:
  81.5 2.6 %copy-start = (f32[1,128]{1,0:T(1,128)S(1)}, f32[1,128]{1,0:T(1,128)}, u32[]{:S(2)}) copy-start(f32[1,128]{1,0:T(1,128)} %get-tuple-element.4) | copy-start | bytes 1540

commit v6 on v5

--- a/solution.py
+++ b/solution.py
@@ -322,11 +322,11 @@
     def spread(k, half):
         dist = (z - k + planes) % planes
 
-        @pl.when(dist <= (3 if k < last else 1))
+        @pl.when(dist <= (3 if k < last else 0))
         def _():
             solved_copy(k, half, to_z_next, 0).start()
 
-        @pl.when((dist == 0) | (dist >= 6) | (dist == (4 if k == last else 0)))
+        @pl.when((dist == 0) | (dist >= 6) | ((dist == 3) | (dist == 4) if k == last else dist == 0))
         def _():
             solved_copy(k, half, to_z_prev, 1).start()
 
@@ -400,7 +400,7 @@
     for k in range(planes):
         dist = (z - k + planes) % planes
         for half in range(2):
-            @pl.when(dist <= (3 if k < last else 1))
+            @pl.when(dist <= (3 if k < last else 0))
             def _():
                 solved_copy(k, half, to_z_next, 0).wait_send()
 
@@ -409,7 +409,7 @@
                 def _():
                     direct_copy(half).wait_send()
 
-            @pl.when((dist == 0) | (dist >= 6) | (dist == (4 if k == last else 0)))
+            @pl.when((dist == 0) | (dist >= 6) | ((dist == 3) | (dist == 4) if k == last else dist == 0))
             def _():
                 solved_copy(k, half, to_z_prev, 1).wait_send()
 

time: 84.8 us -> 88.9 us (1.048)
  the two profiles are of different devices: /device:TPU:36 before, /device:TPU:39 now
where the time goes in v6:
time: 88.9 us; the launch traced here: 88.8 us
  Pallas kernels  85 us (96%)
  other arithmetic  2.62 us (3%)
    pallas_call x1, Pallas kernels, shards(): pl.pallas_call(kernel, out_shape=(jax.ShapeDtypeStruct((1, T), F32), jax....  85 us
    sub x1, other arithmetic, shards(): return (norm_out.reshape(T), z_trail - update)  2.62 us

profile of v6, /device:TPU:39, one launch (start us, length us, event | category | flops | bytes accessed | tf_op | source)
XLA Modules:
  0.0 88.8 jit_solution(11983187304721549140)
XLA Ops:
  0.6 85.0 %panel_update.1 = (f32[1,128]{1,0:T(1,128)}, f32[2048,128]{1,0:T(8,128)}) custom-call(f32[128,2048]{1,0:T(8,128)} %d_hbm.1, f32[128,128]{1,0:T(8,128)} %z_hbm.1, f32[2048,128]{1,0:T(8,128)} %a_hbm.1, f32[1,128]{1,0:T(1,128)} %bitcast.2), custom_call_target="tpu_custom_call" | custom-call | tf_op jit(solution)/shard_map/panel_update/pallas_call | solution.py:420
  85.6 0.0 copy-start
  85.7 2.6 %sub.3 = f32[2048,128]{1,0:T(8,128)} subtract(f32[2048,128]{1,0:T(8,128)} %param.8, f32[2048,128]{1,0:T(8,128)} %get-tuple-element.5) | non-fusion elementwise | flops 262144 | bytes 3145728 | tf_op jit(solution)/shard_map/sub | solution.py:444
  88.3 0.0 copy-done
  88.3 0.5 copy.8
Async XLA Ops:
  85.6 2.6 %copy-start = (f32[1,128]{1,0:T(1,128)S(1)}, f32[1,128]{1,0:T(1,128)}, u32[]{:S(2)}) copy-start(f32[1,128]{1,0:T(1,128)} %get-tuple-element.4) | copy-start | bytes 1540
